TPU v7x, 32 devices: a whole 2x2x4 slice. The times are simulated.
32 devices in a mesh: group: 2 (over y), frame: 4 (over z), space: 2 (over x), head: 2 (over core).
Axes of the slice: x: 2, y: 2, z: 4, core: 2. Of those that a mesh axis runs over, the one named last changes fastest.
Arguments:
- queries: bfloat16 [8, 8, 48, 3072], P(('group', 'frame'), 'space', None, 'head'), parts along dimension 0, may hold values from -8 to 8
- keys: bfloat16 [8, 8, 48, 3072], P(('group', 'frame'), 'space', None, 'head'), parts along dimension 0, may hold values from -8 to 8
- values: bfloat16 [8, 8, 48, 3072], P(('group', 'frame'), 'space', None, 'head'), parts along dimension 0, may hold values from -6 to 6
- flags: int32 [4, 4], replicated, may hold values from 0 to 1, as said below
- widths: int32 [4], replicated, may hold values from 0 to 8, as said below
Outputs:
- attended: bfloat16 [8, 8, 48, 3072], P(('group', 'frame'), 'space', None, 'head'), parts along dimension 0
There are 2 independent parts, one for each index of `group`. A program takes and returns all parts, laid end to end along the dimension named above; an argument that names none is the same for every part. Nothing has to cross between parts.
Inputs may be any that keep to these rules, and one draw needn't show every extreme that they name: flags[f, g] = 1 wherever |f - g| <= 1, and flags[0, 3] = flags[3, 0] = 0. widths[0] = 8, and widths never rise with the frame distance.
All inputs are finite; a program needn't handle non-finite values.
Results may differ from a plain program's by a relative error of at most 0.006.
Values may be sent and summed in bfloat16 or wider, within the bound.
A program may use at most 128 MiB of HBM per device.

v0:
```python
import functools
import math

import jax
import jax.numpy as jnp
from jax import lax
from jax.experimental import pallas as pl
from jax.experimental.pallas import tpu as pltpu
from jax.sharding import PartitionSpec as P

HEAD_DIM = 128
NEG_FILL = -1e30
SCALE = math.log2(math.e) / HEAD_DIM**0.5
MESH = pl.DeviceIdType.MESH


def kernel(
    frames,
    parts,
    heads,
    columns,
    q_ref,
    k_ref,
    v_ref,
    flags_in,
    widths_in,
    out_ref,
    kv,
    qb,
    ob,
    dist,
    wb,
    top,
    total,
    acc,
    local_sem,
    xkv_send,
    xkv_recv,
    xq_send,
    xq_recv,
    z_send,
    z_recv,
    o_local,
    o_send,
    o_recv,
    flags_ref,
    widths_ref,
    table_sem,
):
    frame = lax.axis_index("frame")
    part = lax.axis_index("space")
    rows = q_ref.shape[0]
    tokens = parts * rows
    tile = rows
    far = frames - 2
    LEFT, RIGHT = 0, 1

    def lanes(ref, head):
        return ref.at[:, pl.ds(pl.multiple_of(head * HEAD_DIM, HEAD_DIM), HEAD_DIM)]

    def peer(j):
        return lax.rem(part + j, parts)

    barrier = pltpu.get_barrier_semaphore()
    for j in range(1, parts):
        pl.semaphore_signal(barrier, inc=1, device_id={"space": peer(j)}, device_id_type=MESH)

    @pl.when(frame > 0)
    def _():
        pl.semaphore_signal(barrier, inc=1, device_id={"frame": frame - 1}, device_id_type=MESH)

    @pl.when(frame < frames - 1)
    def _():
        pl.semaphore_signal(barrier, inc=1, device_id={"frame": frame + 1}, device_id_type=MESH)

    def local_copies(h):
        mine = part * heads + h
        return (
            pltpu.make_async_copy(lanes(k_ref, mine), kv.at[frame, h, 0, part], local_sem.at[0, h]),
            pltpu.make_async_copy(lanes(v_ref, mine), kv.at[frame, h, 1, part], local_sem.at[1, h]),
            pltpu.make_async_copy(lanes(q_ref, mine), qb.at[h, part], local_sem.at[2, h]),
        )

    def kv_exchange(h, j, i, src_ref):
        return pltpu.make_async_remote_copy(
            src_ref=lanes(src_ref, peer(j) * heads + h),
            dst_ref=kv.at[frame, h, i, part],
            send_sem=xkv_send.at[i, j - 1, h],
            recv_sem=xkv_recv.at[i, j - 1, h],
            device_id={"space": peer(j)},
            device_id_type=MESH,
        )

    def q_exchange(h, j):
        return pltpu.make_async_remote_copy(
            src_ref=lanes(q_ref, peer(j) * heads + h),
            dst_ref=qb.at[h, part],
            send_sem=xq_send.at[j - 1, h],
            recv_sem=xq_recv.at[j - 1, h],
            device_id={"space": peer(j)},
            device_id_type=MESH,
        )

    def o_exchange(h, j):
        return pltpu.make_async_remote_copy(
            src_ref=ob.at[h, pl.ds(pl.multiple_of(peer(j) * rows, rows), rows)],
            dst_ref=lanes(out_ref, part * heads + h),
            send_sem=o_send.at[j - 1, h],
            recv_sem=o_recv.at[j - 1, h],
            device_id={"space": peer(j)},
            device_id_type=MESH,
        )

    def o_keep(h):
        return pltpu.make_async_copy(
            ob.at[h, pl.ds(pl.multiple_of(part * rows, rows), rows)],
            lanes(out_ref, part * heads + h),
            o_local.at[h],
        )

    def hop(side, step, h, p, i, src=None):
        towards = 1 if side == RIGHT else -1
        owner = frame - towards * (step - 1)
        return pltpu.make_async_remote_copy(
            src_ref=kv.at[owner, h, i, p] if src is None else src,
            dst_ref=kv.at[owner, h, i, p],
            send_sem=z_send.at[side, step - 1, h, p, i],
            recv_sem=z_recv.at[side, step - 1, h, p, i],
            device_id={"frame": frame + towards},
            device_id_type=MESH,
        )

    def can_send(side, step):
        if side == RIGHT:
            return (frame < frames - 1) & (frame - (step - 1) >= 0)
        return (frame > 0) & (frame + (step - 1) <= frames - 1)

    def gets(side, step):
        if side == RIGHT:
            return frame - step >= 0
        return frame + step <= frames - 1

    def landed(side, step, h, p, i):
        towards = 1 if side == RIGHT else -1
        owner = frame - towards * step
        return pltpu.make_async_remote_copy(
            src_ref=kv.at[owner, h, i, p],
            dst_ref=kv.at[owner, h, i, p],
            send_sem=z_send.at[side, step - 1, h, p, i],
            recv_sem=z_recv.at[side, step - 1, h, p, i],
            device_id={"frame": frame - towards},
            device_id_type=MESH,
        )

    def each_head(body):
        @pl.loop(0, heads)
        def _(h):
            body(h)

    pl.semaphore_wait(
        barrier,
        parts - 1 + jnp.where(frame > 0, 1, 0) + jnp.where(frame < frames - 1, 1, 0),
    )

    def open_head(h):
        mine = part * heads + h
        for j in range(1, parts):
            kv_exchange(h, j, 0, k_ref).start()
            kv_exchange(h, j, 1, v_ref).start()
        for side in (LEFT, RIGHT):

            @pl.when(can_send(side, 1))
            def _():
                hop(side, 1, h, part, 0, lanes(k_ref, mine)).start()
                hop(side, 1, h, part, 1, lanes(v_ref, mine)).start()

    each_head(open_head)

    tables = (
        pltpu.make_async_copy(flags_in, flags_ref, table_sem.at[0]),
        pltpu.make_async_copy(widths_in, widths_ref, table_sem.at[1]),
    )
    for copy in tables:
        copy.start()

    def open_queries(h):
        for copy in local_copies(h):
            copy.start()
        for j in range(1, parts):
            q_exchange(h, j).start()

    each_head(open_queries)

    def row_of(axis):
        at = lax.broadcasted_iota(jnp.int32, (tokens, tokens), axis).astype(jnp.float32)
        return jnp.floor((at + 0.5) * (1.0 / columns))

    dist[...] = jnp.abs(row_of(0) - row_of(1))
    top[...] = jnp.full(top.shape, NEG_FILL, jnp.float32)
    total[...] = jnp.zeros(total.shape, jnp.float32)
    acc[...] = jnp.zeros(acc.shape, jnp.float32)

    def pass_parts(h):
        for j in range(1, parts):
            p = lax.rem(part - j + parts, parts)
            for i in (0, 1):
                kv_exchange(h, j, i, (k_ref, v_ref)[i]).wait_recv()
            for side in (LEFT, RIGHT):

                @pl.when(can_send(side, 1))
                def _():
                    for i in (0, 1):
                        hop(side, 1, h, p, i).start()

    each_head(pass_parts)
    for copy in tables:
        copy.wait()

    def masked(h, g, at):
        gap = jnp.abs(frame - g)
        reach = jnp.where(flags_ref[frame, g] > 0, widths_ref[gap], -1).astype(jnp.float32)
        cut = pl.ds(at, tile)
        queries = qb[h].reshape(tokens, HEAD_DIM)[at : at + tile]
        keys = kv[g, h, 0].reshape(tokens, HEAD_DIM)
        scores = lax.dot_general(
            queries, keys, (((1,), (1,)), ((), ())), preferred_element_type=jnp.float32
        )
        scores = jnp.where(dist[cut, :] <= reach, scores, NEG_FILL)
        old_top = top[h, cut]
        new_top = jnp.maximum(old_top, jnp.max(scores, axis=1, keepdims=True))
        weights = jnp.exp2((scores - new_top) * SCALE)
        keep = jnp.exp2((old_top - new_top) * SCALE)
        top[h, cut] = new_top
        total[h, cut] = total[h, cut] * keep + jnp.sum(weights, axis=1, keepdims=True)
        return weights.astype(jnp.bfloat16), keep

    def mixed(weights, h, g):
        vals = kv[g, h, 1].reshape(tokens, HEAD_DIM)
        return jnp.dot(weights, vals, preferred_element_type=jnp.float32)

    def update(h, g):
        for at in range(0, tokens, tile):
            cut = pl.ds(at, tile)
            weights, keep = masked(h, g, at)
            acc[h, cut] = acc[h, cut] * keep + mixed(weights, h, g)

    def await_block(side, step, h, i):
        @pl.when(gets(side, step))
        def _():
            for p in range(parts):
                landed(side, step, h, p, i).wait_recv()

    def source(side, step):
        return frame - step if side == RIGHT else frame + step

    def near(step, h, relay):
        for side in (LEFT, RIGHT):
            for i in (0, 1):
                await_block(side, step, h, i)
            if relay:

                @pl.when(gets(side, step) & can_send(side, step + 1))
                def _():
                    for i in (0, 1):
                        for p in range(parts):
                            hop(side, step + 1, h, p, i).start()

    def blend(step, h):
        for side in (LEFT, RIGHT):

            @pl.when(gets(side, step))
            def _():
                update(h, source(side, step))

    def first(h):
        near(1, h, far > 1)
        for copy in local_copies(h):
            copy.wait()
        for j in range(1, parts):
            q_exchange(h, j).wait_recv()
        update(h, frame)
        blend(1, h)

    each_head(first)

    if far > 2:

        @pl.loop(2, far)
        def _(step):
            def middle(h):
                near(step, h, True)
                blend(step, h)

            each_head(middle)

    def last(h):
        for side in (LEFT, RIGHT):
            if far > 1:
                await_block(side, far, h, 0)

                @pl.when(gets(side, far))
                def _():
                    for at in range(0, tokens, tile):
                        weights, keep = masked(h, source(side, far), at)
                        wb[side, pl.ds(at, tile)] = weights
                        acc[h, pl.ds(at, tile)] = acc[h, pl.ds(at, tile)] * keep

        total[h] = 1.0 / total[h]
        if far > 1:
            for side in (LEFT, RIGHT):
                await_block(side, far, h, 1)

        def finish(p):
            for at in range(0, rows, tile):
                cut = pl.ds(pl.multiple_of(p * rows + at, tile), tile)
                if far > 1:
                    for side in (LEFT, RIGHT):

                        @pl.when(gets(side, far))
                        def _():
                            acc[h, cut] = acc[h, cut] + mixed(
                                wb[side, cut], h, source(side, far)
                            )

                ob[h, cut] = (acc[h, cut] * total[h, cut]).astype(jnp.bfloat16)

        for j in range(1, parts):
            finish(peer(j))
            o_exchange(h, j).start()
        finish(part)
        o_keep(h).start()

    each_head(last)

    def close_head(h):
        o_keep(h).wait()
        for j in range(1, parts):
            o_exchange(h, j).wait()
            q_exchange(h, j).wait_send()
            kv_exchange(h, j, 0, k_ref).wait_send()
            kv_exchange(h, j, 1, v_ref).wait_send()

        @pl.loop(1, far + 1)
        def _(step):
            for side in (LEFT, RIGHT):

                @pl.when(can_send(side, step))
                def _():
                    for p in range(parts):
                        for i in (0, 1):
                            hop(side, step, h, p, i).wait_send()

    each_head(close_head)


def shards(frames, parts, queries, keys, values, flags, widths):
    shape = queries.shape
    columns, features = shape[2], shape[3]
    rows = shape[1] * columns
    heads = features // HEAD_DIM // parts
    tokens = rows * parts
    far = frames - 2
    flat = [a.reshape(rows, features) for a in (queries, keys, values)]
    any_spec = pl.BlockSpec(memory_space=pl.ANY)
    others = max(parts - 1, 1)
    dma = pltpu.SemaphoreType.DMA
    out = pl.pallas_call(
        functools.partial(kernel, frames, parts, heads, columns),
        out_shape=pltpu.VMEM((rows, features), jnp.bfloat16),
        in_specs=[any_spec] * 5,
        out_specs=pl.BlockSpec(memory_space=pltpu.VMEM),
        scratch_shapes=[
            pltpu.VMEM((frames, heads, 2, parts, rows, HEAD_DIM), jnp.bfloat16),
            pltpu.VMEM((heads, parts, rows, HEAD_DIM), jnp.bfloat16),
            pltpu.VMEM((heads, tokens, HEAD_DIM), jnp.bfloat16),
            pltpu.VMEM((tokens, tokens), jnp.float32),
            pltpu.VMEM((2, tokens, tokens), jnp.bfloat16),
            pltpu.VMEM((heads, tokens, 1), jnp.float32),
            pltpu.VMEM((heads, tokens, 1), jnp.float32),
            pltpu.VMEM((heads, tokens, HEAD_DIM), jnp.float32),
            dma((3, heads)),
            dma((2, others, heads)),
            dma((2, others, heads)),
            dma((others, heads)),
            dma((others, heads)),
            dma((2, far, heads, parts, 2)),
            dma((2, far, heads, parts, 2)),
            dma((heads,)),
            dma((others, heads)),
            dma((others, heads)),
            pltpu.SMEM(flags.shape, jnp.int32),
            pltpu.SMEM(widths.shape, jnp.int32),
            dma((2,)),
        ],
        compiler_params=pltpu.CompilerParams(collective_id=0, has_side_effects=True),
    )(*flat, flags, widths)
    return out.reshape(shape)


def solution(mesh):
    spec = P(("group", "frame"), "space", None, "head")
    return jax.shard_map(
        functools.partial(shards, mesh.shape["frame"], mesh.shape["space"]),
        mesh=mesh,
        in_specs=(spec, spec, spec, P(), P()),
        out_specs=spec,
        check_vma=False,
    )
```

profile of v0, /device:TPU:0, one launch (start us, length us, event | category | flops | bytes accessed | tf_op | source)
XLA Modules:
  0.0 62.9 jit_solution(9147277733952223685)
XLA Ops:
  0.0 62.0 %shard_map.55 = bf16[192,1536]{1,0:T(8,128)(2,1)S(1)} custom-call(bf16[192,1536]{1,0:T(8,128)(2,1)} %bitcast.5, bf16[192,1536]{1,0:T(8,128)(2,1)} %bitcast.6, bf16[192,1536]{1,0:T(8,128)(2,1)} %bitcast.7, s32[4,4]{1,0:T(4,128)} %flags_in.1, s32[4]{0:T(128)} %widths_in.1), custom_call_target="tpu_custom_call" | custom-call | tf_op jit(solution)/shard_map/pallas_call | solution.py:367
  62.0 0.8 %copy.7 = bf16[1,4,48,1536]{3,2,1,0:T(8,128)(2,1)} copy(bf16[1,4,48,1536]{3,2,1,0:T(8,128)(2,1)S(1)} %bitcast.4) | data formatting | bytes 1179648
where the time goes:
time: 63 us; the launch traced here: 62.9 us
  Pallas kernels  62 us (98%)
  local copies, waits for them, and re-layouts  0.82 us (1%)
    pallas_call x1, Pallas kernels, shards(): pl.pallas_call(functools.partial(kernel, frames, parts, heads, columns),...  62 us

commit v1 on v0

v1 whole, which is shorter than its diff:
```python
import functools
import math

import jax
import jax.numpy as jnp
from jax import lax
from jax.experimental import pallas as pl
from jax.experimental.pallas import tpu as pltpu
from jax.sharding import PartitionSpec as P

HEAD_DIM = 128
NEG_FILL = -1e30
SCALE = math.log2(math.e) / HEAD_DIM**0.5
MESH = pl.DeviceIdType.MESH
LEFT, RIGHT = 0, 1


def kernel(
    frames,
    parts,
    heads,
    columns,
    q_ref,
    k_ref,
    v_ref,
    flags_in,
    widths_in,
    out_ref,
    kv,
    qb,
    ob,
    dist,
    wb,
    top,
    total,
    acc,
    local_sem,
    x_send,
    x_recv,
    z_send,
    z_recv,
    f_send,
    f_recv,
    o_send,
    o_recv,
    flags_ref,
    widths_ref,
    table_sem,
):
    frame = lax.axis_index("frame")
    part = lax.axis_index("space")
    rows = q_ref.shape[0]
    tokens = parts * rows
    width = heads * HEAD_DIM
    far = frames - 2
    inputs = (k_ref, v_ref, q_ref)

    def lane(head):
        return pl.ds(pl.multiple_of(head * HEAD_DIM, HEAD_DIM), HEAD_DIM)

    def span(p):
        return pl.ds(pl.multiple_of(p * width, HEAD_DIM), width)

    def peer(j):
        return lax.rem(part + j, parts)

    def home(i):
        return qb.at[part] if i == 2 else kv.at[frame, i, part]

    barrier = pltpu.get_barrier_semaphore()
    for j in range(1, parts):
        pl.semaphore_signal(barrier, inc=1, device_id={"space": peer(j)}, device_id_type=MESH)

    @pl.when(frame > 0)
    def _():
        pl.semaphore_signal(barrier, inc=1, device_id={"frame": frame - 1}, device_id_type=MESH)

    @pl.when(frame < frames - 1)
    def _():
        pl.semaphore_signal(barrier, inc=1, device_id={"frame": frame + 1}, device_id_type=MESH)

    def local_copy(i):
        return pltpu.make_async_copy(inputs[i].at[:, span(part)], home(i), local_sem.at[i])

    def exchange(j, i):
        return pltpu.make_async_remote_copy(
            src_ref=inputs[i].at[:, span(peer(j))],
            dst_ref=home(i),
            send_sem=x_send.at[i, j - 1],
            recv_sem=x_recv.at[i, j - 1],
            device_id={"space": peer(j)},
            device_id_type=MESH,
        )

    def o_exchange(h, j):
        return pltpu.make_async_remote_copy(
            src_ref=ob.at[peer(j), :, lane(h)],
            dst_ref=out_ref.at[:, lane(part * heads + h)],
            send_sem=o_send.at[j - 1, h],
            recv_sem=o_recv.at[j - 1, h],
            device_id={"space": peer(j)},
            device_id_type=MESH,
        )

    def towards(side):
        return 1 if side == RIGHT else -1

    def hop(side, step, i, p, src=None, back=False):
        ahead = towards(side)
        owner = frame - ahead * (step if back else step - 1)
        block = kv.at[owner, i, p]
        return pltpu.make_async_remote_copy(
            src_ref=block if src is None else src,
            dst_ref=block,
            send_sem=z_send.at[side, step - 1, i, p],
            recv_sem=z_recv.at[side, step - 1, i, p],
            device_id={"frame": frame - ahead if back else frame + ahead},
            device_id_type=MESH,
        )

    def fine(side, h, back=False):
        ahead = towards(side)
        owner = frame - ahead * (far if back else far - 1)
        block = kv.at[owner, 1, :, :, lane(h)]
        return pltpu.make_async_remote_copy(
            src_ref=block,
            dst_ref=block,
            send_sem=f_send.at[side, h],
            recv_sem=f_recv.at[side, h],
            device_id={"frame": frame - ahead if back else frame + ahead},
            device_id_type=MESH,
        )

    def can_send(side, step):
        if side == RIGHT:
            return (frame < frames - 1) & (frame - (step - 1) >= 0)
        return (frame > 0) & (frame + (step - 1) <= frames - 1)

    def gets(side, step):
        if side == RIGHT:
            return frame - step >= 0
        return frame + step <= frames - 1

    def source(side, step):
        return frame - step if side == RIGHT else frame + step

    def each_head(body):
        @pl.loop(0, heads)
        def _(h):
            body(h)

    pl.semaphore_wait(
        barrier,
        parts - 1 + jnp.where(frame > 0, 1, 0) + jnp.where(frame < frames - 1, 1, 0),
    )

    for i in (0, 1):
        for j in range(1, parts):
            exchange(j, i).start()
        for side in (LEFT, RIGHT):

            @pl.when(can_send(side, 1))
            def _():
                hop(side, 1, i, part, inputs[i].at[:, span(part)]).start()

    tables = (
        pltpu.make_async_copy(flags_in, flags_ref, table_sem.at[0]),
        pltpu.make_async_copy(widths_in, widths_ref, table_sem.at[1]),
    )
    for copy in tables:
        copy.start()
    for i in range(3):
        local_copy(i).start()
    for j in range(1, parts):
        exchange(j, 2).start()

    def row_of(axis):
        at = lax.broadcasted_iota(jnp.int32, (tokens, tokens), axis).astype(jnp.float32)
        return jnp.floor((at + 0.5) * (1.0 / columns))

    dist[...] = jnp.abs(row_of(0) - row_of(1))
    top[...] = jnp.full(top.shape, NEG_FILL, jnp.float32)
    total[...] = jnp.zeros(total.shape, jnp.float32)
    acc[...] = jnp.zeros(acc.shape, jnp.float32)

    def await_piece(side, step, i, p):
        @pl.when(gets(side, step))
        def _():
            hop(side, step, i, p, back=True).wait_recv()

    def relay_piece(side, step, i, p):
        @pl.when(gets(side, step) & can_send(side, step + 1))
        def _():
            hop(side, step + 1, i, p).start()

    def relay_fine(step):
        for side in (LEFT, RIGHT):

            @pl.when(gets(side, step) & can_send(side, step + 1))
            def _():
                each_head(lambda h: fine(side, h).start())

    def pass_piece(i):
        for j in range(1, parts):
            p = lax.rem(part - j + parts, parts)
            exchange(j, i).wait_recv()
            for side in (LEFT, RIGHT):

                @pl.when(can_send(side, 1))
                def _():
                    hop(side, 1, i, p).start()

    def take(step, i, p):
        for side in (LEFT, RIGHT):
            await_piece(side, step, i, p)
            if far > 1:
                relay_piece(side, step, i, p)

    pass_piece(0)
    take(1, 0, part)
    pass_piece(1)
    for copy in tables:
        copy.wait()

    def masked(h, g, p):
        gap = jnp.abs(frame - g)
        reach = jnp.where(flags_ref[frame, g] > 0, widths_ref[gap], -1).astype(jnp.float32)
        cut = pl.ds(p * rows, rows)
        keys = kv[g, 0, :, :, lane(h)].reshape(tokens, HEAD_DIM)
        scores = lax.dot_general(
            qb[p, :, lane(h)], keys, (((1,), (1,)), ((), ())), preferred_element_type=jnp.float32
        )
        scores = jnp.where(dist[cut, :] <= reach, scores, NEG_FILL)
        old_top = top[h, cut]
        new_top = jnp.maximum(old_top, jnp.max(scores, axis=1, keepdims=True))
        weights = jnp.exp2((scores - new_top) * SCALE)
        keep = jnp.exp2((old_top - new_top) * SCALE)
        top[h, cut] = new_top
        total[h, cut] = total[h, cut] * keep + jnp.sum(weights, axis=1, keepdims=True)
        return weights.astype(jnp.bfloat16), keep

    def mixed(weights, h, g):
        vals = kv[g, 1, :, :, lane(h)].reshape(tokens, HEAD_DIM)
        return jnp.dot(weights, vals, preferred_element_type=jnp.float32)

    def update(h, g):
        for p in range(parts):
            cut = pl.ds(p * rows, rows)
            weights, keep = masked(h, g, p)
            acc[h, cut] = acc[h, cut] * keep + mixed(weights, h, g)

    def blend(step):
        def body(h):
            for side in (LEFT, RIGHT):

                @pl.when(gets(side, step))
                def _():
                    update(h, source(side, step))

        each_head(body)

    for j in range(1, parts):
        take(1, 0, peer(j))
    for i in range(3):
        local_copy(i).wait()
    for j in range(1, parts):
        exchange(j, 2).wait_recv()
    each_head(lambda h: update(h, frame))

    def take_values(step):
        for p in range(parts):
            for side in (LEFT, RIGHT):
                await_piece(side, step, 1, p)
                if far > 2:

                    @pl.when(step + 1 < far)
                    def _():
                        relay_piece(side, step, 1, p)

        if far > 1:
            if far == 2:
                relay_fine(step)
            else:

                @pl.when(step + 1 == far)
                def _():
                    relay_fine(step)

    take_values(1)
    blend(1)

    if far > 2:

        @pl.loop(2, far)
        def _(step):
            for p in range(parts):
                take(step, 0, p)
            take_values(step)
            blend(step)

    if far > 1:
        for p in range(parts):
            for side in (LEFT, RIGHT):
                await_piece(side, far, 0, p)

    def last(h):
        if far > 1:
            for side in (LEFT, RIGHT):

                @pl.when(gets(side, far))
                def _():
                    for p in range(parts):
                        cut = pl.ds(p * rows, rows)
                        weights, keep = masked(h, source(side, far), p)
                        wb[side, cut] = weights
                        acc[h, cut] = acc[h, cut] * keep

        total[h] = 1.0 / total[h]
        if far > 1:
            for side in (LEFT, RIGHT):

                @pl.when(gets(side, far))
                def _():
                    fine(side, h, back=True).wait_recv()

        def finish(p):
            cut = pl.ds(pl.multiple_of(p * rows, rows), rows)
            if far > 1:
                for side in (LEFT, RIGHT):

                    @pl.when(gets(side, far))
                    def _():
                        acc[h, cut] = acc[h, cut] + mixed(wb[side, cut], h, source(side, far))

            return (acc[h, cut] * total[h, cut]).astype(jnp.bfloat16)

        for j in range(1, parts):
            ob[peer(j), :, lane(h)] = finish(peer(j))
            o_exchange(h, j).start()
        out_ref[:, lane(part * heads + h)] = finish(part)

    each_head(last)

    def close_head(h):
        for j in range(1, parts):
            o_exchange(h, j).wait()
        if far > 1:
            for side in (LEFT, RIGHT):

                @pl.when(can_send(side, far))
                def _():
                    fine(side, h).wait_send()

    for i in range(3):
        for j in range(1, parts):
            exchange(j, i).wait_send()

    @pl.loop(1, far + 1)
    def _(step):
        for side in (LEFT, RIGHT):

            @pl.when(can_send(side, step))
            def _():
                for p in range(parts):
                    hop(side, step, 0, p).wait_send()

                    @pl.when((step < far) | (step == 1))
                    def _():
                        hop(side, step, 1, p).wait_send()

    each_head(close_head)


def shards(frames, parts, queries, keys, values, flags, widths):
    shape = queries.shape
    columns, features = shape[2], shape[3]
    rows = shape[1] * columns
    heads = features // HEAD_DIM // parts
    tokens = rows * parts
    far = frames - 2
    flat = [a.reshape(rows, features) for a in (queries, keys, values)]
    any_spec = pl.BlockSpec(memory_space=pl.ANY)
    others = max(parts - 1, 1)
    dma = pltpu.SemaphoreType.DMA
    out = pl.pallas_call(
        functools.partial(kernel, frames, parts, heads, columns),
        out_shape=pltpu.VMEM((rows, features), jnp.bfloat16),
        in_specs=[any_spec] * 5,
        out_specs=pl.BlockSpec(memory_space=pltpu.VMEM),
        scratch_shapes=[
            pltpu.VMEM((frames, 2, parts, rows, heads * HEAD_DIM), jnp.bfloat16),
            pltpu.VMEM((parts, rows, heads * HEAD_DIM), jnp.bfloat16),
            pltpu.VMEM((parts, rows, heads * HEAD_DIM), jnp.bfloat16),
            pltpu.VMEM((tokens, tokens), jnp.float32),
            pltpu.VMEM((2, tokens, tokens), jnp.bfloat16),
            pltpu.VMEM((heads, tokens, 1), jnp.float32),
            pltpu.VMEM((heads, tokens, 1), jnp.float32),
            pltpu.VMEM((heads, tokens, HEAD_DIM), jnp.float32),
            dma((3,)),
            dma((3, others)),
            dma((3, others)),
            dma((2, far, 2, parts)),
            dma((2, far, 2, parts)),
            dma((2, heads)),
            dma((2, heads)),
            dma((others, heads)),
            dma((others, heads)),
            pltpu.SMEM(flags.shape, jnp.int32),
            pltpu.SMEM(widths.shape, jnp.int32),
            dma((2,)),
        ],
        compiler_params=pltpu.CompilerParams(collective_id=0, has_side_effects=True),
    )(*flat, flags, widths)
    return out.reshape(shape)


def solution(mesh):
    spec = P(("group", "frame"), "space", None, "head")
    return jax.shard_map(
        functools.partial(shards, mesh.shape["frame"], mesh.shape["space"]),
        mesh=mesh,
        in_specs=(spec, spec, spec, P(), P()),
        out_specs=spec,
        check_vma=False,
    )
```

time: 63 us -> 61.5 us (0.976)
  Pallas kernels: 62 us -> 60.5 us
    pallas_call x1, Pallas kernels: 62 us -> 60.5 us  [shards(): pl.pallas_call(functools.partial(kernel, frames, parts, heads, columns),...]
where the time goes in v1:
time: 61.5 us; the launch traced here: 61.3 us
  Pallas kernels  60.5 us (98%)
  local copies, waits for them, and re-layouts  0.82 us (1%)
    pallas_call x1, Pallas kernels, shards(): pl.pallas_call(functools.partial(kernel, frames, parts, heads, columns),...  60.5 us

profile of v1, /device:TPU:0, one launch (start us, length us, event | category | flops | bytes accessed | tf_op | source)
XLA Modules:
  0.0 61.3 jit_solution(6902862664309279639)
XLA Ops:
  0.0 60.5 %shard_map.55 = bf16[192,1536]{1,0:T(8,128)(2,1)S(1)} custom-call(bf16[192,1536]{1,0:T(8,128)(2,1)} %bitcast.5, bf16[192,1536]{1,0:T(8,128)(2,1)} %bitcast.6, bf16[192,1536]{1,0:T(8,128)(2,1)} %bitcast.7, s32[4,4]{1,0:T(4,128)} %flags_in.1, s32[4]{0:T(128)} %widths_in.1), custom_call_target="tpu_custom_call" | custom-call | tf_op jit(solution)/shard_map/pallas_call | solution.py:385
  60.5 0.8 %copy.7 = bf16[1,4,48,1536]{3,2,1,0:T(8,128)(2,1)} copy(bf16[1,4,48,1536]{3,2,1,0:T(8,128)(2,1)S(1)} %bitcast.4) | data formatting | bytes 1179648

commit v2 on v1

--- a/solution.py
+++ b/solution.py
@@ -222,32 +222,32 @@
     for copy in tables:
         copy.wait()
 
-    def masked(h, g, p):
+    def masked(h, g):
         gap = jnp.abs(frame - g)
         reach = jnp.where(flags_ref[frame, g] > 0, widths_ref[gap], -1).astype(jnp.float32)
-        cut = pl.ds(p * rows, rows)
         keys = kv[g, 0, :, :, lane(h)].reshape(tokens, HEAD_DIM)
+        queries = qb[:, :, lane(h)].reshape(tokens, HEAD_DIM)
         scores = lax.dot_general(
-            qb[p, :, lane(h)], keys, (((1,), (1,)), ((), ())), preferred_element_type=jnp.float32
-        )
-        scores = jnp.where(dist[cut, :] <= reach, scores, NEG_FILL)
-        old_top = top[h, cut]
-        new_top = jnp.maximum(old_top, jnp.max(scores, axis=1, keepdims=True))
+            keys, queries, (((1,), (1,)), ((), ())), preferred_element_type=jnp.float32
+        )
+        scores = jnp.where(dist[...] <= reach, scores, NEG_FILL)
+        old_top = top[h]
+        new_top = jnp.maximum(old_top, jnp.max(scores, axis=0, keepdims=True))
         weights = jnp.exp2((scores - new_top) * SCALE)
         keep = jnp.exp2((old_top - new_top) * SCALE)
-        top[h, cut] = new_top
-        total[h, cut] = total[h, cut] * keep + jnp.sum(weights, axis=1, keepdims=True)
+        top[h] = new_top
+        total[h] = total[h] * keep + jnp.sum(weights, axis=0, keepdims=True)
         return weights.astype(jnp.bfloat16), keep
 
     def mixed(weights, h, g):
         vals = kv[g, 1, :, :, lane(h)].reshape(tokens, HEAD_DIM)
-        return jnp.dot(weights, vals, preferred_element_type=jnp.float32)
+        return lax.dot_general(
+            vals, weights, (((0,), (0,)), ((), ())), preferred_element_type=jnp.float32
+        )
 
     def update(h, g):
-        for p in range(parts):
-            cut = pl.ds(p * rows, rows)
-            weights, keep = masked(h, g, p)
-            acc[h, cut] = acc[h, cut] * keep + mixed(weights, h, g)
+        weights, keep = masked(h, g)
+        acc[h] = acc[h] * keep + mixed(weights, h, g)
 
     def blend(step):
         def body(h):
@@ -309,35 +309,23 @@
 
                 @pl.when(gets(side, far))
                 def _():
-                    for p in range(parts):
-                        cut = pl.ds(p * rows, rows)
-                        weights, keep = masked(h, source(side, far), p)
-                        wb[side, cut] = weights
-                        acc[h, cut] = acc[h, cut] * keep
-
-        total[h] = 1.0 / total[h]
+                    weights, keep = masked(h, source(side, far))
+                    wb[side] = weights
+                    acc[h] = acc[h] * keep
+
         if far > 1:
             for side in (LEFT, RIGHT):
 
                 @pl.when(gets(side, far))
                 def _():
                     fine(side, h, back=True).wait_recv()
-
-        def finish(p):
-            cut = pl.ds(pl.multiple_of(p * rows, rows), rows)
-            if far > 1:
-                for side in (LEFT, RIGHT):
-
-                    @pl.when(gets(side, far))
-                    def _():
-                        acc[h, cut] = acc[h, cut] + mixed(wb[side, cut], h, source(side, far))
-
-            return (acc[h, cut] * total[h, cut]).astype(jnp.bfloat16)
-
+                    acc[h] = acc[h] + mixed(wb[side], h, source(side, far))
+
+        result = jnp.transpose(acc[h] * (1.0 / total[h])).astype(jnp.bfloat16)
+        ob[:, :, lane(h)] = result.reshape(parts, rows, HEAD_DIM)
         for j in range(1, parts):
-            ob[peer(j), :, lane(h)] = finish(peer(j))
             o_exchange(h, j).start()
-        out_ref[:, lane(part * heads + h)] = finish(part)
+        out_ref[:, lane(part * heads + h)] = ob[part, :, lane(h)]
 
     each_head(last)
 
@@ -393,9 +381,9 @@
             pltpu.VMEM((parts, rows, heads * HEAD_DIM), jnp.bfloat16),
             pltpu.VMEM((tokens, tokens), jnp.float32),
             pltpu.VMEM((2, tokens, tokens), jnp.bfloat16),
-            pltpu.VMEM((heads, tokens, 1), jnp.float32),
-            pltpu.VMEM((heads, tokens, 1), jnp.float32),
-            pltpu.VMEM((heads, tokens, HEAD_DIM), jnp.float32),
+            pltpu.VMEM((heads, 1, tokens), jnp.float32),
+            pltpu.VMEM((heads, 1, tokens), jnp.float32),
+            pltpu.VMEM((heads, HEAD_DIM, tokens), jnp.float32),
             dma((3,)),
             dma((3, others)),
             dma((3, others)),

time: 61.5 us -> 61.4 us (level)
  no operation moved by 1% of the time
where the time goes in v2:
time: 61.4 us; the launch traced here: 61.3 us
  Pallas kernels  60.4 us (98%)
  local copies, waits for them, and re-layouts  0.82 us (1%)
    pallas_call x1, Pallas kernels, shards(): pl.pallas_call(functools.partial(kernel, frames, parts, heads, columns),...  60.4 us

profile of v2, /device:TPU:0, one launch (start us, length us, event | category | flops | bytes accessed | tf_op | source)
XLA Modules:
  0.0 61.3 jit_solution(7312658886477292966)
XLA Ops:
  0.0 60.4 %shard_map.55 = bf16[192,1536]{1,0:T(8,128)(2,1)S(1)} custom-call(bf16[192,1536]{1,0:T(8,128)(2,1)} %bitcast.5, bf16[192,1536]{1,0:T(8,128)(2,1)} %bitcast.6, bf16[192,1536]{1,0:T(8,128)(2,1)} %bitcast.7, s32[4,4]{1,0:T(4,128)} %flags_in.1, s32[4]{0:T(128)} %widths_in.1), custom_call_target="tpu_custom_call" | custom-call | tf_op jit(solution)/shard_map/pallas_call | solution.py:373
  60.4 0.8 %copy.7 = bf16[1,4,48,1536]{3,2,1,0:T(8,128)(2,1)} copy(bf16[1,4,48,1536]{3,2,1,0:T(8,128)(2,1)S(1)} %bitcast.4) | data formatting | bytes 1179648
